TPU v7x, 256 devices: a whole 4x4x8 slice. The times are simulated.
256 devices in a mesh: src: 8 (over y, core), tgt: 32 (over z, x).
Axes of the slice: x: 4, y: 4, z: 8, core: 2. Of those that a mesh axis runs over, the one named last changes fastest.
Arguments:
- src_embed: bfloat16 [8192, 256], P('src'), may hold values from -128 to 128
- tgt_embed: bfloat16 [155648, 256], P('tgt'), may hold values from -1 to 1
- qwen_embed: bfloat16 [155648, 256], P('tgt'), may hold values from -6 to 6
- other_log: float32 [155648], P('tgt'), may hold values from -12 to -10
- src_counts: int32 [8192], P('src'), may hold values from 1 to 999
- tgt_counts: int32 [155648], P('tgt'), may hold values from 1 to 999
Outputs:
- transported: float32 [8192, 256], P(('src', 'tgt'))
All inputs are finite; a program needn't handle non-finite values.
Results may differ from a plain program's by a relative error of at most 0.0034.
Values sent between devices are 32-bit elements; how exact they have to be, the bound alone decides.
A program may use at most 128 MiB of HBM per device.

v0:
```python
import jax
import jax.numpy as jnp
from jax import lax
from jax.sharding import PartitionSpec as P

ITERS = 2
inv_temp = 4.0


def logits_of(src_embed, tgt_embed):
    products = lax.dot_general(
        src_embed, tgt_embed, (((1,), (1,)), ((), ())), preferred_element_type=jnp.float32
    )
    return products * inv_temp


def row_lse(values):
    local_peak = jnp.max(values, axis=1)
    peak = lax.pmax(local_peak, "tgt")
    total = lax.psum(jnp.sum(jnp.exp(values - peak[:, None]), axis=1), "tgt")
    return peak + jnp.log(total)


def col_lse(values):
    local_peak = jnp.max(values, axis=0)
    peak = lax.pmax(local_peak, "src")
    total = lax.psum(jnp.sum(jnp.exp(values - peak[None, :]), axis=0), "src")
    return peak + jnp.log(total)


def on_device(src_embed, tgt_embed, qwen_embed, other_log, src_counts, tgt_counts):
    src_float = src_counts.astype(jnp.float32)
    tgt_float = tgt_counts.astype(jnp.float32)
    slab_sum = lax.psum(jnp.sum(src_float), "src")
    vocab_sum = lax.psum(jnp.sum(tgt_float), "tgt")
    src_log = jnp.log(src_float) - jnp.log(slab_sum)
    tgt_log = jnp.log(tgt_float) - jnp.log(vocab_sum)
    stored = logits_of(src_embed, tgt_embed)

    def current():
        return stored

    col_pot = jnp.zeros((tgt_embed.shape[0],), jnp.float32)
    row_pot = jnp.zeros((src_embed.shape[0],), jnp.float32)
    for sweep in range(ITERS):
        row_pot = src_log - row_lse(current() + col_pot[None, :])
        col_pot = tgt_log - jnp.logaddexp(col_lse(current() + row_pot[:, None]), other_log)
    shift = row_pot - src_log
    weights = jnp.exp(shift[:, None] + col_pot[None, :] + current()).astype(jnp.bfloat16)
    owned_rows = src_embed.shape[0] // lax.axis_size("tgt")
    partial_rows = jnp.dot(weights, qwen_embed, preferred_element_type=jnp.float32)
    summed = lax.psum(partial_rows, "tgt")
    return lax.dynamic_slice_in_dim(summed, lax.axis_index("tgt") * owned_rows, owned_rows, 0)


def solution(mesh):
    return jax.shard_map(
        on_device,
        mesh=mesh,
        in_specs=(P("src", None), P("tgt", None), P("tgt", None), P("tgt"), P("src"), P("tgt")),
        out_specs=P(("src", "tgt"), None),
        check_vma=False,
    )
```

profile of v0, /device:TPU:8, one launch (start us, length us, event | category | flops | bytes accessed | tf_op | source)
XLA Modules:
  0.0 646.8 jit_solution(11345955397474943461)
XLA Ops:
  6.5 0.0 copy-start
  6.5 0.0 all-reduce.3.cloned.1.call-start
  6.5 1.5 convert_reduce_fusion
  8.0 1.3 convert_reduce_fusion.1
  9.3 0.0 copy-done
  9.3 0.0 copy-start.3
  9.3 9.3 %fusion.4 = (f32[1024]{0:T(1024)S(1)}, f32[1024,4864]{1,0:T(8,128)}) fusion(bf16[1024,256]{1,0:T(8,128)(2,1)} %param.6, bf16[4864,256]{1,0:T(8,128)(2,1)S(1)} %copy-done), kind=kOutput, calls=%fused_computation.24 | convolution fusion | flops 2560097280 | bytes 22941696 | tf_op jit(solution)/shard_map/dot_general | solution.py:11
  18.7 77.7 %pmax.28 = f32[1024]{0:T(1024)S(1)} all-reduce(f32[1024]{0:T(1024)S(1)} %get-tuple-element.9), channel_id=1, replica_groups=mesh['src'=8,'tgt'=32] {'tgt'}, use_global_device_ids=true, to_apply=%region_5.0 | all-reduce | flops 1024 | bytes 8192 | tf_op jit(solution)/shard_map/pmax | solution.py:19
  96.3 10.6 %psum.49 = f32[]{:T(128)} all-reduce(f32[]{:T(128)} %convert_reduce_fusion.1), channel_id=1, replica_groups=mesh['src'=8,'tgt'=32] {'src'}, use_global_device_ids=true, to_apply=%region_1.0 | all-reduce | flops 1 | bytes 8 | tf_op jit(solution)/shard_map/psum | solution.py:34
  107.7 9.4 %exponential_reduce_fusion.3 = f32[1024]{0:T(1024)S(1)} fusion(f32[1024,4864]{1,0:T(8,128)} %get-tuple-element.10, f32[1024]{0:T(1024)S(1)} %pmax.28), kind=kLoop, calls=%fused_computation.4 | loop fusion | flops 9960448 | bytes 19931136 | tf_op jit(solution)/shard_map/reduce_sum | solution.py:20
  117.1 71.1 %all-reduce = (f32[1024]{0:T(1024)S(1)}, f32[]{:T(128)}) all-reduce(f32[1024]{0:T(1024)S(1)} %exponential_reduce_fusion.3, f32[]{:T(128)} %convert_reduce_fusion), channel_id=1, replica_groups=mesh['src'=8,'tgt'=32] {'tgt'}, use_global_device_ids=true, to_apply=%region_7.0 | all-reduce | flops 1025 | bytes 8200 | tf_op jit(solution)/shard_map/psum | solution.py:20
  188.2 0.0 copy-done.3
  188.2 0.0 copy-start.1
  188.2 0.0 copy-start.2
  188.2 8.3 %add_reduce_fusion.2 = f32[4864]{0:T(1024)S(1)} fusion(f32[1024,4864]{1,0:T(8,128)} %get-tuple-element.10, f32[1024]{0:T(1024)S(1)} %add_subtract_fusion.1), kind=kLoop, calls=%fused_computation.7 | loop fusion | flops 9956608 | bytes 19946496 | tf_op jit(solution)/shard_map/reduce_max | solution.py:25
  196.5 23.0 %pmax.29 = f32[4864]{0:T(1024)S(1)} all-reduce(f32[4864]{0:T(1024)S(1)} %add_reduce_fusion.2), channel_id=1, replica_groups=mesh['src'=8,'tgt'=32] {'src'}, use_global_device_ids=true, to_apply=%region_9.0 | all-reduce | flops 4864 | bytes 38912 | tf_op jit(solution)/shard_map/pmax | solution.py:26
  219.5 10.9 %exponential_reduce_fusion.2 = f32[4864]{0:T(1024)S(1)} fusion(f32[1024,4864]{1,0:T(8,128)} %get-tuple-element.10, f32[4864]{0:T(1024)S(1)} %pmax.29, f32[1024]{0:T(1024)S(1)} %add_subtract_fusion.1), kind=kLoop, calls=%fused_computation.3 | loop fusion | flops 14937344 | bytes 19965952 | tf_op jit(solution)/shard_map/reduce_sum | solution.py:27
  230.4 23.8 %psum.52 = f32[4864]{0:T(1024)S(1)} all-reduce(f32[4864]{0:T(1024)S(1)} %exponential_reduce_fusion.2), channel_id=1, replica_groups=mesh['src'=8,'tgt'=32] {'src'}, use_global_device_ids=true, to_apply=%region_11.0 | all-reduce | flops 4864 | bytes 38912 | tf_op jit(solution)/shard_map/psum | solution.py:27
  254.9 0.0 copy-done.1
  254.9 0.0 copy-done.2
  254.9 8.1 %add_reduce_fusion.1 = f32[1024]{0:T(1024)S(1)} fusion(f32[1024,4864]{1,0:T(8,128)} %get-tuple-element.10, f32[4864]{0:T(1024)S(1)} %select_subtract_fusion.1), kind=kLoop, calls=%fused_computation.6 | loop fusion | flops 9960448 | bytes 19946496 | tf_op jit(solution)/shard_map/reduce_max | solution.py:18
  263.0 71.6 %pmax.30 = f32[1024]{0:T(1024)S(1)} all-reduce(f32[1024]{0:T(1024)S(1)} %add_reduce_fusion.1), channel_id=1, replica_groups=mesh['src'=8,'tgt'=32] {'tgt'}, use_global_device_ids=true, to_apply=%region_13.0 | all-reduce | flops 1024 | bytes 8192 | tf_op jit(solution)/shard_map/pmax | solution.py:19
  334.6 10.0 %exponential_reduce_fusion.1 = f32[1024]{0:T(1024)S(1)} fusion(f32[1024,4864]{1,0:T(8,128)} %get-tuple-element.10, f32[1024]{0:T(1024)S(1)} %pmax.30, f32[4864]{0:T(1024)S(1)} %select_subtract_fusion.1), kind=kLoop, calls=%fused_computation.2 | loop fusion | flops 14941184 | bytes 19950592 | tf_op jit(solution)/shard_map/reduce_sum | solution.py:20
  344.7 69.6 %psum.53 = f32[1024]{0:T(1024)S(1)} all-reduce(f32[1024]{0:T(1024)S(1)} %exponential_reduce_fusion.1), channel_id=1, replica_groups=mesh['src'=8,'tgt'=32] {'tgt'}, use_global_device_ids=true, to_apply=%region_15.0 | all-reduce | flops 1024 | bytes 8192 | tf_op jit(solution)/shard_map/psum | solution.py:20
  414.3 8.3 %add_reduce_fusion = f32[4864]{0:T(1024)S(1)} fusion(f32[1024,4864]{1,0:T(8,128)} %get-tuple-element.10, f32[1024]{0:T(1024)S(1)} %get-tuple-element.8), kind=kLoop, calls=%fused_computation.5 | loop fusion | flops 9956608 | bytes 19946496 | tf_op jit(solution)/shard_map/reduce_max | solution.py:25
  422.6 23.6 %pmax.31 = f32[4864]{0:T(1024)S(1)} all-reduce(f32[4864]{0:T(1024)S(1)} %add_reduce_fusion), channel_id=1, replica_groups=mesh['src'=8,'tgt'=32] {'src'}, use_global_device_ids=true, to_apply=%region_17.0 | all-reduce | flops 4864 | bytes 38912 | tf_op jit(solution)/shard_map/pmax | solution.py:26
  446.2 10.9 %exponential_reduce_fusion = f32[4864]{0:T(1024)S(1)} fusion(f32[1024,4864]{1,0:T(8,128)} %get-tuple-element.10, f32[4864]{0:T(1024)S(1)} %pmax.31, f32[1024]{0:T(1024)S(1)} %get-tuple-element.8), kind=kLoop, calls=%fused_computation.1 | loop fusion | flops 14937344 | bytes 19965952 | tf_op jit(solution)/shard_map/reduce_sum | solution.py:27
  457.1 23.8 %psum.54 = f32[4864]{0:T(1024)S(1)} all-reduce(f32[4864]{0:T(1024)S(1)} %exponential_reduce_fusion), channel_id=1, replica_groups=mesh['src'=8,'tgt'=32] {'src'}, use_global_device_ids=true, to_apply=%region_19.0 | all-reduce | flops 4864 | bytes 38912 | tf_op jit(solution)/shard_map/psum | solution.py:27
  480.9 11.5 %fusion = f32[1024,256]{1,0:T(8,128)} fusion(bf16[4864,256]{1,0:T(8,128)(2,1)} %param.8, f32[1024,4864]{1,0:T(8,128)} %get-tuple-element.10, f32[4864]{0:T(1024)S(1)} %select_subtract_fusion, f32[1024]{0:T(1024)S(1)} %get-tuple-element.7), kind=kOutput, calls=%fused_computation.9 | convolution fusion | flops 2565079040 | bytes 23485440 | tf_op jit(solution)/shard_map/dot_general | solution.py:51
  492.4 0.0 all-reduce.3.cloned.1.call-update
  492.5 146.1 %all-reduce.3.cloned.1.call-done = f32[1024,256]{1,0:T(8,128)} async-done(((f32[1024,256]{1,0:T(8,128)}), f32[1024,256]{1,0:T(8,128)}) %all-reduce.3.cloned.1.call-update) | async-done | bytes 1048592 | tf_op jit(solution)/shard_map/psum | solution.py:52
  638.6 1.4 constant_dynamic-slice_fusion
  (4 shorter events, 0.1 us)
Async XLA Ops:
  6.5 2.8 copy-start
  6.5 632.0 %all-reduce.3.cloned.1.call-start = ((), (), s32[]{:S(2)}) async-start(), calls=%async_computation | async-start | bytes 2097152 | tf_op jit(solution)/shard_map/psum | solution.py:52
  9.3 178.9 %copy-start.3 = (s32[1024]{0:T(1024)S(1)}, s32[1024]{0:T(1024)}, u32[]{:S(2)}) copy-start(s32[1024]{0:T(1024)} %param.10) | copy-start | bytes 12292
  188.2 66.7 %copy-start.1 = (s32[4864]{0:T(1024)S(1)}, s32[4864]{0:T(1024)}, u32[]{:S(2)}) copy-start(s32[4864]{0:T(1024)} %param.11) | copy-start | bytes 58372
  188.2 66.7 %copy-start.2 = (f32[4864]{0:T(1024)S(1)}, f32[4864]{0:T(1024)}, u32[]{:S(2)}) copy-start(f32[4864]{0:T(1024)} %param.9) | copy-start | bytes 58372
Sparse Core Ops, SparseCore 0:
  492.6 145.9 all-reduce.2
where the time goes:
time: 647 us
  blocking collectives  395 us (61%)
  waiting for transfers between devices  146 us (23%)
  other arithmetic  68.7 us (11%)
  matrix products  20.8 us (3%)
  between operations  14.8 us (2%)
    pmax x2, blocking collectives, row_lse(): peak = lax.pmax(local_peak, 'tgt')  149 us
    psum x1, waiting for transfers between devices, on_device(): summed = lax.psum(partial_rows, 'tgt')  146 us
    psum x2, blocking collectives, row_lse(): total = lax.psum(jnp.sum(jnp.exp(values - peak[:, None]), axis=1), 'tgt')  141 us
    psum x2, blocking collectives, col_lse(): total = lax.psum(jnp.sum(jnp.exp(values - peak[None, :]), axis=0), 'src')  47.6 us
    pmax x2, blocking collectives, col_lse(): peak = lax.pmax(local_peak, 'src')  46.6 us
    reduce_sum x2, other arithmetic, col_lse(): total = lax.psum(jnp.sum(jnp.exp(values - peak[None, :]), axis=0), 'src')  21.7 us
    reduce_sum x2, other arithmetic, row_lse(): total = lax.psum(jnp.sum(jnp.exp(values - peak[:, None]), axis=1), 'tgt')  19.4 us
    reduce_max x2, other arithmetic, col_lse(): local_peak = jnp.max(values, axis=0)  16.6 us
  transfers between devices with their start and end apart: 1, of which 1 were waited for; matrix products, arithmetic and copies ran while one was open for 0% of the time, Pallas kernels for 0%

commit v1 on v0

--- a/solution.py
+++ b/solution.py
@@ -24,7 +24,8 @@
 def col_lse(values):
     local_peak = jnp.max(values, axis=0)
     peak = lax.pmax(local_peak, "src")
-    total = lax.psum(jnp.sum(jnp.exp(values - peak[None, :]), axis=0), "src")
+    z_in = jnp.sum(jnp.exp(values - peak[None, :]), axis=0)
+    total = lax.all_gather(z_in, "src").sum(axis=0)
     return peak + jnp.log(total)
 
 

time: 647 us -> 627 us (0.969)
  blocking collectives: 395 us -> 374 us
    psum x2 -> x0, blocking collectives: 47.6 us -> none  [col_lse(): total = lax.psum(jnp.sum(jnp.exp(values - peak[None, :]), axis=0), 'src')]
    all_gather x0 -> x2, blocking collectives: none -> 26.3 us  [col_lse(): total = lax.all_gather(z_in, 'src').sum(axis=0)]
    reduce_sum x2 -> x4, other arithmetic: 21.7 us -> 22 us  [the longest x2 21.7 us: col_lse(): z_in = jnp.sum(jnp.exp(values - peak[None, :]), axis=0)]
where the time goes in v1:
time: 627 us; the launch traced here: 626 us
  blocking collectives  374 us (60%)
  waiting for transfers between devices  147 us (23%)
  other arithmetic  68.9 us (11%)
  matrix products  20.8 us (3%)
  between operations  14.9 us (2%)
    pmax x2, blocking collectives, row_lse(): peak = lax.pmax(local_peak, 'tgt')  149 us
    psum x1, waiting for transfers between devices, on_device(): summed = lax.psum(partial_rows, 'tgt')  147 us
    psum x2, blocking collectives, row_lse(): total = lax.psum(jnp.sum(jnp.exp(values - peak[:, None]), axis=1), 'tgt')  141 us
    pmax x2, blocking collectives, col_lse(): peak = lax.pmax(local_peak, 'src')  46.5 us
    all_gather x2, blocking collectives, col_lse(): total = lax.all_gather(z_in, 'src').sum(axis=0)  26.3 us
    reduce_sum x2, other arithmetic, col_lse(): z_in = jnp.sum(jnp.exp(values - peak[None, :]), axis=0)  21.7 us
    reduce_sum x2, other arithmetic, row_lse(): total = lax.psum(jnp.sum(jnp.exp(values - peak[:, None]), axis=1), 'tgt')  19.4 us
    reduce_max x2, other arithmetic, col_lse(): local_peak = jnp.max(values, axis=0)  16.6 us
  transfers between devices with their start and end apart: 1, of which 1 were waited for; matrix products, arithmetic and copies ran while one was open for 0% of the time, Pallas kernels for 0%

profile of v1, /device:TPU:8, one launch (start us, length us, event | category | flops | bytes accessed | tf_op | source)
XLA Modules:
  0.0 626.4 jit_solution(881737695912126949)
XLA Ops:
  6.5 0.0 copy-start
  6.5 0.0 all-reduce.3.cloned.1.call-start
  6.5 1.5 convert_reduce_fusion
  8.0 1.3 convert_reduce_fusion.1
  9.3 0.0 copy-done
  9.3 0.0 copy-start.3
  9.3 9.3 %fusion.4 = (f32[1024]{0:T(1024)S(1)}, f32[1024,4864]{1,0:T(8,128)}) fusion(bf16[1024,256]{1,0:T(8,128)(2,1)} %param.6, bf16[4864,256]{1,0:T(8,128)(2,1)S(1)} %copy-done), kind=kOutput, calls=%fused_computation.24 | convolution fusion | flops 2560097280 | bytes 22941696 | tf_op jit(solution)/shard_map/dot_general | solution.py:11
  18.7 77.7 %pmax.28 = f32[1024]{0:T(1024)S(1)} all-reduce(f32[1024]{0:T(1024)S(1)} %get-tuple-element.9), channel_id=1, replica_groups=mesh['src'=8,'tgt'=32] {'tgt'}, use_global_device_ids=true, to_apply=%region_5.0 | all-reduce | flops 1024 | bytes 8192 | tf_op jit(solution)/shard_map/pmax | solution.py:19
  96.3 10.6 %psum.35 = f32[]{:T(128)} all-reduce(f32[]{:T(128)} %convert_reduce_fusion.1), channel_id=1, replica_groups=mesh['src'=8,'tgt'=32] {'src'}, use_global_device_ids=true, to_apply=%region_1.0 | all-reduce | flops 1 | bytes 8 | tf_op jit(solution)/shard_map/psum | solution.py:35
  107.7 9.4 %exponential_reduce_fusion.3 = f32[1024]{0:T(1024)S(1)} fusion(f32[1024,4864]{1,0:T(8,128)} %get-tuple-element.10, f32[1024]{0:T(1024)S(1)} %pmax.28), kind=kLoop, calls=%fused_computation.4 | loop fusion | flops 9960448 | bytes 19931136 | tf_op jit(solution)/shard_map/reduce_sum | solution.py:20
  117.1 71.1 %all-reduce = (f32[1024]{0:T(1024)S(1)}, f32[]{:T(128)}) all-reduce(f32[1024]{0:T(1024)S(1)} %exponential_reduce_fusion.3, f32[]{:T(128)} %convert_reduce_fusion), channel_id=1, replica_groups=mesh['src'=8,'tgt'=32] {'tgt'}, use_global_device_ids=true, to_apply=%region_7.0 | all-reduce | flops 1025 | bytes 8200 | tf_op jit(solution)/shard_map/psum | solution.py:20
  188.2 0.0 copy-done.3
  188.2 0.0 copy-start.1
  188.2 0.0 copy-start.2
  188.2 8.3 %add_reduce_fusion.2 = f32[4864]{0:T(1024)S(1)} fusion(f32[1024,4864]{1,0:T(8,128)} %get-tuple-element.10, f32[1024]{0:T(1024)S(1)} %add_subtract_fusion.1), kind=kLoop, calls=%fused_computation.7 | loop fusion | flops 9956608 | bytes 19946496 | tf_op jit(solution)/shard_map/reduce_max | solution.py:25
  196.5 23.0 %pmax.29 = f32[4864]{0:T(1024)S(1)} all-reduce(f32[4864]{0:T(1024)S(1)} %add_reduce_fusion.2), channel_id=1, replica_groups=mesh['src'=8,'tgt'=32] {'src'}, use_global_device_ids=true, to_apply=%region_9.0 | all-reduce | flops 4864 | bytes 38912 | tf_op jit(solution)/shard_map/pmax | solution.py:26
  219.5 10.9 %exponential_reduce_fusion.2 = f32[4864]{0:T(1024)S(1)} fusion(f32[1024,4864]{1,0:T(8,128)} %get-tuple-element.10, f32[4864]{0:T(1024)S(1)} %pmax.29, f32[1024]{0:T(1024)S(1)} %add_subtract_fusion.1), kind=kLoop, calls=%fused_computation.3 | loop fusion | flops 14937344 | bytes 19965952 | tf_op jit(solution)/shard_map/reduce_sum | solution.py:27
  230.4 13.2 %all-gather.2 = f32[8,1,4864]{2,1,0:T(1,128)S(1)} all-gather(f32[1,1,4864]{2,1,0:T(1,128)S(1)} %reshape.11), channel_id=2, replica_groups=mesh['src'=8,'tgt'=32] {'src'}, dimensions={0}, use_global_device_ids=true | all-gather | bytes 175104 | tf_op jit(solution)/shard_map/all_gather | solution.py:28
  244.4 0.1 reduce_sum.76
  244.5 0.0 copy-done.1
  244.5 0.0 copy-done.2
  244.6 8.1 %add_reduce_fusion.1 = f32[1024]{0:T(1024)S(1)} fusion(f32[1024,4864]{1,0:T(8,128)} %get-tuple-element.10, f32[4864]{0:T(1024)S(1)} %select_subtract_fusion.1), kind=kLoop, calls=%fused_computation.6 | loop fusion | flops 9960448 | bytes 19946496 | tf_op jit(solution)/shard_map/reduce_max | solution.py:18
  252.6 71.6 %pmax.30 = f32[1024]{0:T(1024)S(1)} all-reduce(f32[1024]{0:T(1024)S(1)} %add_reduce_fusion.1), channel_id=1, replica_groups=mesh['src'=8,'tgt'=32] {'tgt'}, use_global_device_ids=true, to_apply=%region_13.0 | all-reduce | flops 1024 | bytes 8192 | tf_op jit(solution)/shard_map/pmax | solution.py:19
  324.2 10.0 %exponential_reduce_fusion.1 = f32[1024]{0:T(1024)S(1)} fusion(f32[1024,4864]{1,0:T(8,128)} %get-tuple-element.10, f32[1024]{0:T(1024)S(1)} %pmax.30, f32[4864]{0:T(1024)S(1)} %select_subtract_fusion.1), kind=kLoop, calls=%fused_computation.2 | loop fusion | flops 14941184 | bytes 19950592 | tf_op jit(solution)/shard_map/reduce_sum | solution.py:20
  334.3 69.7 %psum.38 = f32[1024]{0:T(1024)S(1)} all-reduce(f32[1024]{0:T(1024)S(1)} %exponential_reduce_fusion.1), channel_id=1, replica_groups=mesh['src'=8,'tgt'=32] {'tgt'}, use_global_device_ids=true, to_apply=%region_15.0 | all-reduce | flops 1024 | bytes 8192 | tf_op jit(solution)/shard_map/psum | solution.py:20
  403.9 8.3 %add_reduce_fusion = f32[4864]{0:T(1024)S(1)} fusion(f32[1024,4864]{1,0:T(8,128)} %get-tuple-element.10, f32[1024]{0:T(1024)S(1)} %get-tuple-element.8), kind=kLoop, calls=%fused_computation.5 | loop fusion | flops 9956608 | bytes 19946496 | tf_op jit(solution)/shard_map/reduce_max | solution.py:25
  412.2 23.5 %pmax.31 = f32[4864]{0:T(1024)S(1)} all-reduce(f32[4864]{0:T(1024)S(1)} %add_reduce_fusion), channel_id=1, replica_groups=mesh['src'=8,'tgt'=32] {'src'}, use_global_device_ids=true, to_apply=%region_17.0 | all-reduce | flops 4864 | bytes 38912 | tf_op jit(solution)/shard_map/pmax | solution.py:26
  435.7 10.9 %exponential_reduce_fusion = f32[4864]{0:T(1024)S(1)} fusion(f32[1024,4864]{1,0:T(8,128)} %get-tuple-element.10, f32[4864]{0:T(1024)S(1)} %pmax.31, f32[1024]{0:T(1024)S(1)} %get-tuple-element.8), kind=kLoop, calls=%fused_computation.1 | loop fusion | flops 14937344 | bytes 19965952 | tf_op jit(solution)/shard_map/reduce_sum | solution.py:27
  446.6 13.1 %all-gather.3 = f32[8,1,4864]{2,1,0:T(1,128)S(1)} all-gather(f32[1,1,4864]{2,1,0:T(1,128)S(1)} %reshape.13), channel_id=3, replica_groups=mesh['src'=8,'tgt'=32] {'src'}, dimensions={0}, use_global_device_ids=true | all-gather | bytes 175104 | tf_op jit(solution)/shard_map/all_gather | solution.py:28
  459.7 0.1 reduce_sum.79
  459.9 11.5 %fusion = f32[1024,256]{1,0:T(8,128)} fusion(bf16[4864,256]{1,0:T(8,128)(2,1)} %param.8, f32[1024,4864]{1,0:T(8,128)} %get-tuple-element.10, f32[4864]{0:T(1024)S(1)} %select_subtract_fusion, f32[1024]{0:T(1024)S(1)} %get-tuple-element.7), kind=kOutput, calls=%fused_computation.9 | convolution fusion | flops 2565079040 | bytes 23485440 | tf_op jit(solution)/shard_map/dot_general | solution.py:52
  471.4 0.0 all-reduce.3.cloned.1.call-update
  471.4 146.8 %all-reduce.3.cloned.1.call-done = f32[1024,256]{1,0:T(8,128)} async-done(((f32[1024,256]{1,0:T(8,128)}), f32[1024,256]{1,0:T(8,128)}) %all-reduce.3.cloned.1.call-update) | async-done | bytes 1048592 | tf_op jit(solution)/shard_map/psum | solution.py:53
  618.2 1.4 constant_dynamic-slice_fusion
  (6 shorter events, 0.1 us)
Async XLA Ops:
  6.5 2.8 copy-start
  6.5 611.7 %all-reduce.3.cloned.1.call-start = ((), (), s32[]{:S(2)}) async-start(), calls=%async_computation | async-start | bytes 2097152 | tf_op jit(solution)/shard_map/psum | solution.py:53
  9.3 178.9 %copy-start.3 = (s32[1024]{0:T(1024)S(1)}, s32[1024]{0:T(1024)}, u32[]{:S(2)}) copy-start(s32[1024]{0:T(1024)} %param.10) | copy-start | bytes 12292
  188.2 56.3 %copy-start.1 = (s32[4864]{0:T(1024)S(1)}, s32[4864]{0:T(1024)}, u32[]{:S(2)}) copy-start(s32[4864]{0:T(1024)} %param.11) | copy-start | bytes 58372
  188.2 56.3 %copy-start.2 = (f32[4864]{0:T(1024)S(1)}, f32[4864]{0:T(1024)}, u32[]{:S(2)}) copy-start(f32[4864]{0:T(1024)} %param.9) | copy-start | bytes 58372
Sparse Core Ops, SparseCore 0:
  471.5 146.6 all-reduce.2
